TPU v7x, 512 devices: a whole 4x4x16 slice. The times are simulated.
512 devices in a mesh: vec: 64 (over y, z), row: 8 (over x, core).
Axes of the slice: x: 4, y: 4, z: 16, core: 2. Of those that a mesh axis runs over, the one named last changes fastest.
Arguments:
- vectors: bfloat16 [8, 4096, 1024], P('row', 'vec'), may hold values from -6 to 6
- rotation: bfloat16 [1024, 1024], P(None, 'vec'), may hold values from -0.1875 to 0.1875
- blocks: bfloat16 [256, 8, 128, 128], P('row'), may hold values from -0.125 to 0.125
- column_blocks: int32 [256, 8], P('row'), may hold values from -2 to 257, as said below
Outputs:
- filtered: bfloat16 [8, 4096, 1024], P('row', 'vec')
Inputs may be any that keep to these rules, and one draw needn't show every extreme that they name: `column_blocks`: block row r of partition p = r // 32 lists 8 distinct column blocks between p * 32 - 2 and p * 32 + 33; the first block row of every partition lists the lowest of these and the last one the highest; column blocks outside 0 to 255 stand for zeros.
All inputs are finite; a program needn't handle non-finite values.
Results may differ from a plain program's by a relative error of at most 0.006.
Values may be sent and summed in bfloat16 or wider, within the bound.
A program may use at most 64 MiB of HBM per device.

v0:
```python
import jax
import jax.numpy as jnp
from jax import lax
from jax.sharding import PartitionSpec as P

BS = 128
HB = 2
STEPS = 4
centre = 0.3
half_width = 1.2


def with_halo(block, sides, width):
    for axis, dim in sides:
        count = lax.axis_size(axis)
        forward = [(i, i + 1) for i in range(count - 1)]
        backward = [(target, source) for source, target in forward]
        low = lax.ppermute(
            lax.slice_in_dim(block, block.shape[dim] - width, None, axis=dim), axis, forward
        )
        high = lax.ppermute(lax.slice_in_dim(block, 0, width, axis=dim), axis, backward)
        block = jnp.concatenate([low, block, high], axis=dim)
    return block


def apply_matrix(operand, blocks, offsets):
    extended = with_halo(operand, (("row", 1),), HB * BS)
    stacked = extended.reshape(extended.shape[0], -1, BS)
    picked = stacked[:, offsets]
    product = jnp.einsum("rjab,krjb->kra", blocks, picked, preferred_element_type=jnp.float32)
    return product.reshape(extended.shape[0], -1)


def filter_panel(vec_panel, blocks, offsets):
    previous = vec_panel.astype(jnp.float32)
    current = (apply_matrix(vec_panel, blocks, offsets) - centre * previous) / half_width
    for turn_index in range(STEPS - 1):
        operand = current.astype(jnp.bfloat16)
        following = (
            2.0 * (apply_matrix(operand, blocks, offsets) - centre * current) / half_width
            - previous
        )
        previous = current
        current = following
    return current.astype(jnp.bfloat16)


def local(vectors, rotation, blocks, column_blocks):
    local_rows = vectors[0]
    offsets = column_blocks - (lax.axis_index("row") * column_blocks.shape[0] - HB)
    contract = (((0,), (1,)), ((), ()))
    vec_panel = lax.dot_general(
        rotation,
        lax.all_gather(local_rows, "vec", axis=0, tiled=True),
        contract,
        preferred_element_type=jnp.float32,
    ).astype(jnp.bfloat16)
    filtered = filter_panel(vec_panel, blocks, offsets)
    returned = lax.all_to_all(filtered, "vec", split_axis=1, concat_axis=0, tiled=True)
    return jnp.transpose(returned)[None]


def solution(mesh):
    placed = (P("row", "vec", None), P(None, "vec"), P("row", None, None, None), P("row", None))
    return jax.shard_map(
        local, mesh=mesh, in_specs=placed, out_specs=P("row", "vec", None), check_vma=False
    )
```

profile of v0, /device:TPU:1, one launch (start us, length us, event | category | flops | bytes accessed | tf_op | source)
XLA Modules:
  0.0 266.6 jit_solution(13129486595092253713)
XLA Ops:
  6.5 0.0 copy-start
  6.5 0.0 all-gather.3.cloned.1.call-start
  6.5 0.7 all-gather.3.cloned.1.call-update
  7.3 0.7 compare_select_fusion
  8.0 0.1 copy.14
  8.0 0.1 reshape.37
  8.1 156.6 %all-gather.3.cloned.1.call-done = bf16[1,4096,1024]{2,1,0:T(8,128)(2,1)} async-done(((bf16[1,64,1024]{2,1,0:T(8,128)(2,1)}), bf16[1,4096,1024]{2,1,0:T(8,128)(2,1)}) %all-gather.3.cloned.1.call-update) | async-done | bytes 8388624 | tf_op jit(solution)/shard_map/all_gather | solution.py:54
  164.7 0.0 copy-done
  164.7 5.7 %fusion.2 = bf16[16,4096]{1,0:T(8,128)(2,1)S(1)} fusion(bf16[1024,16]{0,1:T(8,128)(2,1)S(1)} %copy-done, bf16[1,4096,1024]{2,1,0:T(8,128)(2,1)} %all-gather.3.cloned.1.call-done), kind=kOutput, calls=%fused_computation.6 | convolution fusion | flops 134283264 | bytes 8552448 | tf_op jit(solution)/shard_map/dot_general | solution.py:52
  170.4 11.5 %collective-permute-start = (bf16[16,256]{1,0:T(8,128)(2,1)S(1)}, bf16[16,256]{1,0:T(8,128)(2,1)S(1)}, u32[]{:S(2)}, u32[]{:S(2)}) collective-permute-start(bf16[16,256]{1,0:T(8,128)(2,1)S(1)} %get-tuple-element.11), channel_id=1, source_target_pairs={{0,1},{1,2},{2,3},{3,4},{4,5},{5,6},{6,7},{8,9},{9,10},{10,11},{11... | collective-permute-start | bytes 24584 | tf_op jit(solution)/shard_map/ppermute | solution.py:18
  181.8 1.9 collective-permute-start.1
  183.8 0.0 collective-permute-done
  183.8 3.0 %collective-permute-done.1 = bf16[16,256]{1,0:T(8,128)(2,1)S(1)} collective-permute-done((bf16[16,256]{1,0:T(8,128)(2,1)S(1)}, bf16[16,256]{1,0:T(8,128)(2,1)S(1)}, u32[]{:S(2)}, u32[]{:S(2)}) %collective-permute-start.1) | collective-permute-done | bytes 8224 | tf_op jit(solution)/shard_map/ppermute | solution.py:21
  186.8 0.8 gather_fusion
  187.7 5.7 %convolution_bitcast_fusion.3 = f32[32,2,8,128]{3,2,1,0:T(8,128)S(1)} fusion(bf16[16,32,8,128]{3,0,2,1:T(8,128)(2,1)S(1)} %bitcast.130, bf16[32,8,128,128]{3,2,1,0:T(8,128)(2,1)} %param.6), kind=kOutput, calls=%fused_computation.10 | convolution fusion | flops 134217728 | bytes 9699328 | tf_op jit(solution)/shard_map/rjab,krjb->kra/dot_general | solution.py:30
  193.4 0.1 multiply_convert_fusion
  193.4 1.9 collective-permute-start.2
  195.4 2.4 collective-permute-start.3
  197.8 0.0 collective-permute-done.2
  197.8 2.6 collective-permute-done.3
  200.4 0.8 gather_fusion.1
  201.2 5.7 %convolution_bitcast_fusion.2 = f32[32,2,8,128]{3,2,1,0:T(8,128)S(1)} fusion(bf16[16,32,8,128]{3,0,2,1:T(8,128)(2,1)S(1)} %bitcast.131, bf16[32,8,128,128]{3,2,1,0:T(8,128)(2,1)} %param.6), kind=kOutput, calls=%fused_computation.9 | convolution fusion | flops 134217728 | bytes 9699328 | tf_op jit(solution)/shard_map/rjab,krjb->kra/dot_general | solution.py:30
  206.9 0.1 fusion.13
  207.0 1.9 collective-permute-start.4
  209.0 2.4 collective-permute-start.5
  211.3 0.0 collective-permute-done.4
  211.4 2.6 collective-permute-done.5
  214.0 0.8 gather_fusion.2
  214.8 5.7 %convolution_bitcast_fusion.1 = f32[32,2,8,128]{3,2,1,0:T(8,128)S(1)} fusion(bf16[16,32,8,128]{3,0,2,1:T(8,128)(2,1)S(1)} %bitcast.132, bf16[32,8,128,128]{3,2,1,0:T(8,128)(2,1)} %param.6), kind=kOutput, calls=%fused_computation.8 | convolution fusion | flops 134217728 | bytes 9699328 | tf_op jit(solution)/shard_map/rjab,krjb->kra/dot_general | solution.py:30
  220.5 0.1 fusion.12
  220.6 1.9 collective-permute-start.6
  222.6 2.4 collective-permute-start.7
  225.0 0.0 collective-permute-done.6
  225.0 2.6 collective-permute-done.7
  227.6 0.8 gather_fusion.3
  228.4 5.7 %convolution_bitcast_fusion = f32[32,2,8,128]{3,2,1,0:T(8,128)S(1)} fusion(bf16[16,32,8,128]{3,0,2,1:T(8,128)(2,1)S(1)} %bitcast.129, bf16[32,8,128,128]{3,2,1,0:T(8,128)(2,1)} %param.6), kind=kOutput, calls=%fused_computation.7 | convolution fusion | flops 134217728 | bytes 9699328 | tf_op jit(solution)/shard_map/rjab,krjb->kra/dot_general | solution.py:30
  234.1 0.2 fusion.8
  234.3 0.2 all_to_all.14
  234.5 0.2 copy.72
  234.7 0.2 reshape.80
  234.9 23.9 %all_to_all.19 = bf16[64,2,512]{2,1,0:T(2,128)(2,1)S(1)} all-to-all(bf16[64,2,512]{2,1,0:T(2,128)(2,1)S(1)} %reshape.80), channel_id=1, replica_groups=mesh['vec'=64,'row'=8] {'vec'}, dimensions={0} | all-to-all | bytes 262144 | tf_op jit(solution)/shard_map/all_to_all | solution.py:59
  258.8 0.2 reshape.81
  259.0 0.8 copy.24
  (9 shorter events, 0.1 us)
Async XLA Ops:
  6.5 158.2 %copy-start = (bf16[1024,16]{0,1:T(8,128)(2,1)S(1)}, bf16[1024,16]{0,1:T(8,128)(2,1)}, u32[]{:S(2)}) copy-start(bf16[1024,16]{0,1:T(8,128)(2,1)} %param.5) | copy-start | bytes 98308
  6.5 158.2 %all-gather.3.cloned.1.call-start = ((), (), s32[]{:S(2)}) async-start(), calls=%async_computation.1 | async-start | bytes 8519680 | tf_op jit(solution)/shard_map/all_gather | solution.py:54
  170.4 13.4 %collective-permute-start = (bf16[16,256]{1,0:T(8,128)(2,1)S(1)}, bf16[16,256]{1,0:T(8,128)(2,1)S(1)}, u32[]{:S(2)}, u32[]{:S(2)}) collective-permute-start(bf16[16,256]{1,0:T(8,128)(2,1)S(1)} %get-tuple-element.11), channel_id=1, source_target_pairs={{0,1},{1,2},{2,3},{3,4},{4,5},{5,6},{6,7},{8,9},{9,10},{10,11},{11... | collective-permute-start | bytes 24584 | tf_op jit(solution)/shard_map/ppermute | solution.py:18
  181.8 5.0 %collective-permute-start.1 = (bf16[16,256]{1,0:T(8,128)(2,1)S(1)}, bf16[16,256]{1,0:T(8,128)(2,1)S(1)}, u32[]{:S(2)}, u32[]{:S(2)}) collective-permute-start(bf16[16,256]{1,0:T(8,128)(2,1)S(1)} %get-tuple-element.12), channel_id=1, source_target_pairs={{1,0},{2,1},{3,2},{4,3},{5,4},{6,5},{7,6},{9,8},{10,9},{11,10},{12... | collective-permute-start | bytes 24584 | tf_op jit(solution)/shard_map/ppermute | solution.py:21
  193.4 4.3 %collective-permute-start.2 = (bf16[16,256]{1,0:T(8,128)(2,1)S(1)}, bf16[16,256]{1,0:T(8,128)(2,1)S(1)}, u32[]{:S(2)}, u32[]{:S(2)}) collective-permute-start(bf16[16,256]{1,0:T(8,128)(2,1)S(1)} %get-tuple-element.9), channel_id=1, source_target_pairs={{0,1},{1,2},{2,3},{3,4},{4,5},{5,6},{6,7},{8,9},{9,10},{10,11},{11... | collective-permute-start | bytes 24584 | tf_op jit(solution)/shard_map/ppermute | solution.py:18
  195.4 5.0 %collective-permute-start.3 = (bf16[16,256]{1,0:T(8,128)(2,1)S(1)}, bf16[16,256]{1,0:T(8,128)(2,1)S(1)}, u32[]{:S(2)}, u32[]{:S(2)}) collective-permute-start(bf16[16,256]{1,0:T(8,128)(2,1)S(1)} %get-tuple-element.10), channel_id=1, source_target_pairs={{1,0},{2,1},{3,2},{4,3},{5,4},{6,5},{7,6},{9,8},{10,9},{11,10},{12... | collective-permute-start | bytes 24584 | tf_op jit(solution)/shard_map/ppermute | solution.py:21
  207.0 4.3 %collective-permute-start.4 = (bf16[16,256]{1,0:T(8,128)(2,1)S(1)}, bf16[16,256]{1,0:T(8,128)(2,1)S(1)}, u32[]{:S(2)}, u32[]{:S(2)}) collective-permute-start(bf16[16,256]{1,0:T(8,128)(2,1)S(1)} %get-tuple-element.7), channel_id=1, source_target_pairs={{0,1},{1,2},{2,3},{3,4},{4,5},{5,6},{6,7},{8,9},{9,10},{10,11},{11... | collective-permute-start | bytes 24584 | tf_op jit(solution)/shard_map/ppermute | solution.py:18
  209.0 5.0 %collective-permute-start.5 = (bf16[16,256]{1,0:T(8,128)(2,1)S(1)}, bf16[16,256]{1,0:T(8,128)(2,1)S(1)}, u32[]{:S(2)}, u32[]{:S(2)}) collective-permute-start(bf16[16,256]{1,0:T(8,128)(2,1)S(1)} %get-tuple-element.8), channel_id=1, source_target_pairs={{1,0},{2,1},{3,2},{4,3},{5,4},{6,5},{7,6},{9,8},{10,9},{11,10},{12... | collective-permute-start | bytes 24584 | tf_op jit(solution)/shard_map/ppermute | solution.py:21
  220.6 4.3 %collective-permute-start.6 = (bf16[16,256]{1,0:T(8,128)(2,1)S(1)}, bf16[16,256]{1,0:T(8,128)(2,1)S(1)}, u32[]{:S(2)}, u32[]{:S(2)}) collective-permute-start(bf16[16,256]{1,0:T(8,128)(2,1)S(1)} %get-tuple-element.5), channel_id=1, source_target_pairs={{0,1},{1,2},{2,3},{3,4},{4,5},{5,6},{6,7},{8,9},{9,10},{10,11},{11... | collective-permute-start | bytes 24584 | tf_op jit(solution)/shard_map/ppermute | solution.py:18
  222.6 5.0 %collective-permute-start.7 = (bf16[16,256]{1,0:T(8,128)(2,1)S(1)}, bf16[16,256]{1,0:T(8,128)(2,1)S(1)}, u32[]{:S(2)}, u32[]{:S(2)}) collective-permute-start(bf16[16,256]{1,0:T(8,128)(2,1)S(1)} %get-tuple-element.6), channel_id=1, source_target_pairs={{1,0},{2,1},{3,2},{4,3},{5,4},{6,5},{7,6},{9,8},{10,9},{11,10},{12... | collective-permute-start | bytes 24584 | tf_op jit(solution)/shard_map/ppermute | solution.py:21
Sparse Core Ops, SparseCore 0:
  10.3 154.3 all-gather.2
where the time goes:
time: 267 us
  waiting for transfers between devices  168 us (63%)
  matrix products  28.3 us (11%)
  starting transfers between devices  26.3 us (10%)
  blocking collectives  23.9 us (9%)
  between operations  13.6 us (5%)
  local copies, waits for them, and re-layouts  5.19 us (2%)
    all_gather x1, waiting for transfers between devices, local(): lax.all_gather(local_rows, 'vec', axis=0, tiled=True)  157 us
    all_to_all x1, blocking collectives, local(): lax.all_to_all(filtered, 'vec', split_axis=1, concat_axis=0, tiled=True)  23.9 us
    dot_general x4, matrix products, apply_matrix(): jnp.einsum('rjab,krjb->kra', blocks, picked, preferred_element_type=jnp.f...  22.6 us
    ppermute x4, starting transfers between devices, with_halo(): lax.ppermute(lax.slice_in_dim(block, block.shape[dim] - width, None, axis...  17.3 us
    ppermute x4, waiting for transfers between devices, with_halo(): lax.ppermute(lax.slice_in_dim(block, 0, width, axis=dim), axis, backward)  10.7 us
    ppermute x4, starting transfers between devices, with_halo(): lax.ppermute(lax.slice_in_dim(block, 0, width, axis=dim), axis, backward)  9.05 us
    dot_general x1, matrix products, local(): lax.dot_general(rotation, lax.all_gather(local_rows, 'vec', axis=0, tiled...  5.65 us
  transfers between devices with their start and end apart: 9, of which 5 were waited for; matrix products, arithmetic and copies ran while one was open for 0% of the time, Pallas kernels for 0%

commit v1 on v0

--- a/solution.py
+++ b/solution.py
@@ -1,3 +1,4 @@
+import functools
 import jax
 import jax.numpy as jnp
 from jax import lax
@@ -8,6 +9,23 @@
 STEPS = 4
 centre = 0.3
 half_width = 1.2
+
+
+def fill_members_all(v0, mesh_dim):
+    a_next = lax.axis_size(mesh_dim)
+    piece_next = lax.axis_index(mesh_dim)
+    right_arr, out_arr = (a_next, piece_next)
+    mid_arr, u1 = (v0, 1)
+    while u1 < right_arr:
+        field_out = lax.ppermute(mid_arr, mesh_dim, [(m, m ^ u1) for m in range(right_arr)])
+        shaped = jnp.concatenate([mid_arr, field_out], axis=0)
+        base_arr = jnp.concatenate([field_out, mid_arr], axis=0)
+        mid_arr = jnp.where(out_arr & u1 == 0, shaped, base_arr)
+        u1 = 2 * u1
+    return mid_arr
+
+
+rest_the_task = functools.partial(fill_members_all, mesh_dim="vec")
 
 
 def with_halo(block, sides, width):
@@ -50,10 +68,7 @@
     offsets = column_blocks - (lax.axis_index("row") * column_blocks.shape[0] - HB)
     contract = (((0,), (1,)), ((), ()))
     vec_panel = lax.dot_general(
-        rotation,
-        lax.all_gather(local_rows, "vec", axis=0, tiled=True),
-        contract,
-        preferred_element_type=jnp.float32,
+        rotation, rest_the_task(local_rows), contract, preferred_element_type=jnp.float32
     ).astype(jnp.bfloat16)
     filtered = filter_panel(vec_panel, blocks, offsets)
     returned = lax.all_to_all(filtered, "vec", split_axis=1, concat_axis=0, tiled=True)

time: 267 us -> 425 us (1.59)
  waiting for transfers between devices: 168 us -> 240 us
  starting transfers between devices: 26.3 us -> 87.5 us
  blocking collectives: 23.9 us -> 52 us
  between operations: 13.6 us -> 0.38 us
  other arithmetic: 1.24 us -> 9.61 us
    ppermute x0 -> x6, waiting for transfers between devices: none -> 229 us  [fill_members_all(): lax.ppermute(mid_arr, mesh_dim, [(m, m ^ u1) for m in range(right_arr)])]
    all_gather x1 -> x0, waiting for transfers between devices: 157 us -> none  [local(): lax.all_gather(local_rows, 'vec', axis=0, tiled=True)]
    ppermute x0 -> x6, starting transfers between devices: none -> 67.3 us  [fill_members_all(): lax.ppermute(mid_arr, mesh_dim, [(m, m ^ u1) for m in range(right_arr)])]
    all_to_all x1, blocking collectives: 23.9 us -> 52 us  [local(): lax.all_to_all(filtered, 'vec', split_axis=1, concat_axis=0, tiled=True)]
    select_n x0 -> x5, other arithmetic: none -> 9.06 us  [fill_members_all(): mid_arr = jnp.where(out_arr & u1 == 0, shaped, base_arr)]
    ppermute x4, starting transfers between devices: 17.3 us -> 11.1 us  [with_halo(): lax.ppermute(lax.slice_in_dim(block, block.shape[dim] - width, None, axis...]
  transfers between devices with their start and end apart: 9 -> 14, of which waited for: 5 -> 10; matrix products, arithmetic and copies ran while one was open for 0% -> 0% of each run, Pallas kernels for 0% -> 0%
where the time goes in v1:
time: 425 us; the launch traced here: 424 us
  waiting for transfers between devices  240 us (56%)
  starting transfers between devices  87.5 us (21%)
  blocking collectives  52 us (12%)
  matrix products  29.7 us (7%)
  other arithmetic  9.61 us (2%)
  local copies, waits for them, and re-layouts  5.19 us (1%)
    ppermute x6, waiting for transfers between devices, fill_members_all(): lax.ppermute(mid_arr, mesh_dim, [(m, m ^ u1) for m in range(right_arr)])  229 us
    ppermute x6, starting transfers between devices, fill_members_all(): lax.ppermute(mid_arr, mesh_dim, [(m, m ^ u1) for m in range(right_arr)])  67.3 us
    all_to_all x1, blocking collectives, local(): lax.all_to_all(filtered, 'vec', split_axis=1, concat_axis=0, tiled=True)  52 us
    dot_general x4, matrix products, apply_matrix(): jnp.einsum('rjab,krjb->kra', blocks, picked, preferred_element_type=jnp.f...  22.6 us
    ppermute x4, starting transfers between devices, with_halo(): lax.ppermute(lax.slice_in_dim(block, block.shape[dim] - width, None, axis...  11.1 us
    ppermute x4, waiting for transfers between devices, with_halo(): lax.ppermute(lax.slice_in_dim(block, 0, width, axis=dim), axis, backward)  10.7 us
    select_n x5, other arithmetic, fill_members_all(): mid_arr = jnp.where(out_arr & u1 == 0, shaped, base_arr)  9.06 us
    ppermute x4, starting transfers between devices, with_halo(): lax.ppermute(lax.slice_in_dim(block, 0, width, axis=dim), axis, backward)  9.05 us
  transfers between devices with their start and end apart: 14, of which 10 were waited for; matrix products, arithmetic and copies ran while one was open for 0% of the time, Pallas kernels for 0%

profile of v1, /device:TPU:1, one launch (start us, length us, event | category | flops | bytes accessed | tf_op | source)
XLA Modules:
  0.0 423.9 jit_solution(4378814530193492054)
XLA Ops:
  0.0 0.0 copy-start
  0.0 4.5 %collective-permute-start = (bf16[64,1024]{1,0:T(8,128)(2,1)}, bf16[64,1024]{1,0:T(8,128)(2,1)S(1)}, u32[]{:S(2)}, u32[]{:S(2)}) collective-permute-start(bf16[64,1024]{1,0:T(8,128)(2,1)} %bitcast.133), channel_id=1, source_target_pairs={{0,8},{8,0},{16,24},{24,16},{32,40},{40,32},{48,56},{56,48},{64,72... | collective-permute-start | bytes 393224 | tf_op jit(solution)/shard_map/ppermute | solution.py:20
  4.5 2.5 collective-permute-done
  7.1 1.0 maximum_select_fusion.10
  8.1 5.7 %collective-permute-start.1 = (bf16[128,1024]{1,0:T(8,128)(2,1)S(1)}, bf16[128,1024]{1,0:T(8,128)(2,1)S(1)}, u32[]{:S(2)}, u32[]{:S(2)}) collective-permute-start(bf16[128,1024]{1,0:T(8,128)(2,1)S(1)} %maximum_select_fusion.10), channel_id=1, source_target_pairs={{0,16},{8,24},{16,0},{24,8},{32,48},{40,56},{48,32},{56,40},{64,80... | collective-permute-start | bytes 786440 | tf_op jit(solution)/shard_map/ppermute | solution.py:20
  13.8 6.6 %collective-permute-done.1 = bf16[128,1024]{1,0:T(8,128)(2,1)S(1)} collective-permute-done((bf16[128,1024]{1,0:T(8,128)(2,1)S(1)}, bf16[128,1024]{1,0:T(8,128)(2,1)S(1)}, u32[]{:S(2)}, u32[]{:S(2)}) %collective-permute-start.1) | collective-permute-done | bytes 262176 | tf_op jit(solution)/shard_map/ppermute | solution.py:20
  20.3 0.1 maximum_select_fusion.9
  20.5 13.6 %collective-permute-start.2 = (bf16[256,1024]{1,0:T(8,128)(2,1)S(1)}, bf16[256,1024]{1,0:T(8,128)(2,1)S(1)}, u32[]{:S(2)}, u32[]{:S(2)}) collective-permute-start(bf16[256,1024]{1,0:T(8,128)(2,1)S(1)} %maximum_select_fusion.9), channel_id=1, source_target_pairs={{0,32},{8,40},{16,48},{24,56},{32,0},{40,8},{48,16},{56,24},{64,96... | collective-permute-start | bytes 1572872 | tf_op jit(solution)/shard_map/ppermute | solution.py:20
  34.1 45.1 %collective-permute-done.2 = bf16[256,1024]{1,0:T(8,128)(2,1)S(1)} collective-permute-done((bf16[256,1024]{1,0:T(8,128)(2,1)S(1)}, bf16[256,1024]{1,0:T(8,128)(2,1)S(1)}, u32[]{:S(2)}, u32[]{:S(2)}) %collective-permute-start.2) | collective-permute-done | bytes 524320 | tf_op jit(solution)/shard_map/ppermute | solution.py:20
  79.1 0.5 maximum_select_fusion.8
  79.6 35.6 %collective-permute-start.3 = (bf16[512,1024]{1,0:T(8,128)(2,1)S(1)}, bf16[512,1024]{1,0:T(8,128)(2,1)}, u32[]{:S(2)}, u32[]{:S(2)}) collective-permute-start(bf16[512,1024]{1,0:T(8,128)(2,1)S(1)} %maximum_select_fusion.8), channel_id=1, source_target_pairs={{0,64},{8,72},{16,80},{24,88},{32,96},{40,104},{48,112},{56,120},{... | collective-permute-start | bytes 3145736 | tf_op jit(solution)/shard_map/ppermute | solution.py:20
  115.2 39.8 %collective-permute-done.3 = bf16[512,1024]{1,0:T(8,128)(2,1)} collective-permute-done((bf16[512,1024]{1,0:T(8,128)(2,1)S(1)}, bf16[512,1024]{1,0:T(8,128)(2,1)}, u32[]{:S(2)}, u32[]{:S(2)}) %collective-permute-start.3) | collective-permute-done | bytes 1048608 | tf_op jit(solution)/shard_map/ppermute | solution.py:20
  155.0 2.5 maximum_select_fusion.7
  157.5 3.2 collective-permute-start.4
  160.7 0.0 copy-start.1
  160.7 45.5 %collective-permute-done.4 = bf16[1024,1024]{1,0:T(8,128)(2,1)} collective-permute-done((bf16[1024,1024]{1,0:T(8,128)(2,1)S(1)}, bf16[1024,1024]{1,0:T(8,128)(2,1)}, u32[]{:S(2)}, u32[]{:S(2)}) %collective-permute-start.4) | collective-permute-done | bytes 2097184 | tf_op jit(solution)/shard_map/ppermute | solution.py:20
  206.2 4.9 %maximum_select_fusion.6 = bf16[2048,1024]{1,0:T(8,128)(2,1)} fusion(bf16[1024,1024]{1,0:T(8,128)(2,1)} %collective-permute-done.4, bf16[1024,1024]{1,0:T(8,128)(2,1)S(1)} %maximum_select_fusion.7, pred[]{:T(512)S(6)} %eq.19), kind=kLoop, calls=%fused_computation.14 | loop fusion | flops 18874368 | bytes 8388609 | tf_op jit(solution)/shard_map/jit(_where)/select_n | solution.py:23
  211.1 4.8 %collective-permute-start.5 = (bf16[2048,1024]{1,0:T(8,128)(2,1)}, bf16[2048,1024]{1,0:T(8,128)(2,1)}, u32[]{:S(2)}, u32[]{:S(2)}) collective-permute-start(bf16[2048,1024]{1,0:T(8,128)(2,1)} %maximum_select_fusion.6), channel_id=1, source_target_pairs={{0,256},{8,264},{16,272},{24,280},{32,288},{40,296},{48,304},{56,3... | collective-permute-start | bytes 12582920 | tf_op jit(solution)/shard_map/ppermute | solution.py:20
  215.9 0.0 copy-done.1
  215.9 0.1 copy.14
  216.0 0.1 reshape.37
  216.1 89.4 %collective-permute-done.5 = bf16[2048,1024]{1,0:T(8,128)(2,1)} collective-permute-done((bf16[2048,1024]{1,0:T(8,128)(2,1)}, bf16[2048,1024]{1,0:T(8,128)(2,1)}, u32[]{:S(2)}, u32[]{:S(2)}) %collective-permute-start.5) | collective-permute-done | bytes 4194336 | tf_op jit(solution)/shard_map/ppermute | solution.py:20
  305.5 0.0 copy-done
  305.5 7.1 %fusion.8 = bf16[16,4096]{1,0:T(8,128)(2,1)S(1)} fusion(bf16[1024,16]{0,1:T(8,128)(2,1)S(1)} %copy-done, bf16[2048,1024]{1,0:T(8,128)(2,1)} %collective-permute-done.5, bf16[2048,1024]{1,0:T(8,128)(2,1)} %maximum_select_fusion.6, pred[]{:T(512)S(6)} %eq.18), kind=kOutput, calls=%fused_computation.13 | convolution fusion | flops 172032000 | bytes 8552449 | tf_op jit(solution)/shard_map/dot_general | solution.py:70
  312.6 5.3 %collective-permute-start.6 = (bf16[16,256]{1,0:T(8,128)(2,1)S(1)}, bf16[16,256]{1,0:T(8,128)(2,1)S(1)}, u32[]{:S(2)}, u32[]{:S(2)}) collective-permute-start(bf16[16,256]{1,0:T(8,128)(2,1)S(1)} %get-tuple-element.11), channel_id=1, source_target_pairs={{0,1},{1,2},{2,3},{3,4},{4,5},{5,6},{6,7},{8,9},{9,10},{10,11},{11... | collective-permute-start | bytes 24584 | tf_op jit(solution)/shard_map/ppermute | solution.py:36
  317.9 1.9 collective-permute-start.7
  319.8 0.0 collective-permute-done.6
  319.8 3.0 collective-permute-done.7
  322.9 0.8 gather_fusion
  323.7 5.7 %convolution_bitcast_fusion.3 = f32[32,2,8,128]{3,2,1,0:T(8,128)S(1)} fusion(bf16[16,32,8,128]{3,0,2,1:T(8,128)(2,1)S(1)} %bitcast.128, bf16[32,8,128,128]{3,2,1,0:T(8,128)(2,1)} %param.6), kind=kOutput, calls=%fused_computation.19 | convolution fusion | flops 134217728 | bytes 9699328 | tf_op jit(solution)/shard_map/rjab,krjb->kra/dot_general | solution.py:48
  329.4 0.1 multiply_convert_fusion
  329.5 1.9 collective-permute-start.8
  331.4 2.4 collective-permute-start.9
  333.8 0.0 collective-permute-done.8
  333.8 2.6 collective-permute-done.9
  336.4 0.8 gather_fusion.1
  337.3 5.7 %convolution_bitcast_fusion.2 = f32[32,2,8,128]{3,2,1,0:T(8,128)S(1)} fusion(bf16[16,32,8,128]{3,0,2,1:T(8,128)(2,1)S(1)} %bitcast.129, bf16[32,8,128,128]{3,2,1,0:T(8,128)(2,1)} %param.6), kind=kOutput, calls=%fused_computation.18 | convolution fusion | flops 134217728 | bytes 9699328 | tf_op jit(solution)/shard_map/rjab,krjb->kra/dot_general | solution.py:48
  342.9 0.1 fusion.18
  343.0 1.9 collective-permute-start.10
  345.0 2.4 collective-permute-start.11
  347.4 0.0 collective-permute-done.10
  347.4 2.6 collective-permute-done.11
  350.0 0.8 gather_fusion.2
  350.8 5.7 %convolution_bitcast_fusion.1 = f32[32,2,8,128]{3,2,1,0:T(8,128)S(1)} fusion(bf16[16,32,8,128]{3,0,2,1:T(8,128)(2,1)S(1)} %bitcast.130, bf16[32,8,128,128]{3,2,1,0:T(8,128)(2,1)} %param.6), kind=kOutput, calls=%fused_computation.17 | convolution fusion | flops 134217728 | bytes 9699328 | tf_op jit(solution)/shard_map/rjab,krjb->kra/dot_general | solution.py:48
  356.5 0.1 fusion.17
  356.6 1.9 collective-permute-start.12
  358.6 2.4 collective-permute-start.13
  361.0 0.0 collective-permute-done.12
  361.0 2.6 collective-permute-done.13
  363.6 0.8 gather_fusion.3
  364.4 5.7 %convolution_bitcast_fusion = f32[32,2,8,128]{3,2,1,0:T(8,128)S(1)} fusion(bf16[16,32,8,128]{3,0,2,1:T(8,128)(2,1)S(1)} %bitcast.127, bf16[32,8,128,128]{3,2,1,0:T(8,128)(2,1)} %param.6), kind=kOutput, calls=%fused_computation.16 | convolution fusion | flops 134217728 | bytes 9699328 | tf_op jit(solution)/shard_map/rjab,krjb->kra/dot_general | solution.py:48
  370.1 0.2 fusion.12
  370.3 0.2 all_to_all.14
  370.5 0.2 copy.72
  370.7 0.2 reshape.79
  370.9 52.0 %all_to_all.19 = bf16[64,2,512]{2,1,0:T(2,128)(2,1)S(1)} all-to-all(bf16[64,2,512]{2,1,0:T(2,128)(2,1)S(1)} %reshape.79), channel_id=1, replica_groups=mesh['vec'=64,'row'=8] {'vec'}, dimensions={0} | all-to-all | bytes 262144 | tf_op jit(solution)/shard_map/all_to_all | solution.py:74
  422.9 0.2 reshape.80
  423.1 0.8 copy.24
  (10 shorter events, 0.1 us)
Async XLA Ops:
  0.0 305.5 %copy-start = (bf16[1024,16]{0,1:T(8,128)(2,1)S(1)}, bf16[1024,16]{0,1:T(8,128)(2,1)}, u32[]{:S(2)}) copy-start(bf16[1024,16]{0,1:T(8,128)(2,1)} %param.5) | copy-start | bytes 98308
  0.0 7.1 %collective-permute-start = (bf16[64,1024]{1,0:T(8,128)(2,1)}, bf16[64,1024]{1,0:T(8,128)(2,1)S(1)}, u32[]{:S(2)}, u32[]{:S(2)}) collective-permute-start(bf16[64,1024]{1,0:T(8,128)(2,1)} %bitcast.133), channel_id=1, source_target_pairs={{0,8},{8,0},{16,24},{24,16},{32,40},{40,32},{48,56},{56,48},{64,72... | collective-permute-start | bytes 393224 | tf_op jit(solution)/shard_map/ppermute | solution.py:20
  8.1 12.2 %collective-permute-start.1 = (bf16[128,1024]{1,0:T(8,128)(2,1)S(1)}, bf16[128,1024]{1,0:T(8,128)(2,1)S(1)}, u32[]{:S(2)}, u32[]{:S(2)}) collective-permute-start(bf16[128,1024]{1,0:T(8,128)(2,1)S(1)} %maximum_select_fusion.10), channel_id=1, source_target_pairs={{0,16},{8,24},{16,0},{24,8},{32,48},{40,56},{48,32},{56,40},{64,80... | collective-permute-start | bytes 786440 | tf_op jit(solution)/shard_map/ppermute | solution.py:20
  20.5 58.7 %collective-permute-start.2 = (bf16[256,1024]{1,0:T(8,128)(2,1)S(1)}, bf16[256,1024]{1,0:T(8,128)(2,1)S(1)}, u32[]{:S(2)}, u32[]{:S(2)}) collective-permute-start(bf16[256,1024]{1,0:T(8,128)(2,1)S(1)} %maximum_select_fusion.9), channel_id=1, source_target_pairs={{0,32},{8,40},{16,48},{24,56},{32,0},{40,8},{48,16},{56,24},{64,96... | collective-permute-start | bytes 1572872 | tf_op jit(solution)/shard_map/ppermute | solution.py:20
  79.6 75.3 %collective-permute-start.3 = (bf16[512,1024]{1,0:T(8,128)(2,1)S(1)}, bf16[512,1024]{1,0:T(8,128)(2,1)}, u32[]{:S(2)}, u32[]{:S(2)}) collective-permute-start(bf16[512,1024]{1,0:T(8,128)(2,1)S(1)} %maximum_select_fusion.8), channel_id=1, source_target_pairs={{0,64},{8,72},{16,80},{24,88},{32,96},{40,104},{48,112},{56,120},{... | collective-permute-start | bytes 3145736 | tf_op jit(solution)/shard_map/ppermute | solution.py:20
  157.5 48.7 %collective-permute-start.4 = (bf16[1024,1024]{1,0:T(8,128)(2,1)S(1)}, bf16[1024,1024]{1,0:T(8,128)(2,1)}, u32[]{:S(2)}, u32[]{:S(2)}) collective-permute-start(bf16[1024,1024]{1,0:T(8,128)(2,1)S(1)} %maximum_select_fusion.7), channel_id=1, source_target_pairs={{0,128},{8,136},{16,144},{24,152},{32,160},{40,168},{48,176},{56,1... | collective-permute-start | bytes 6291464 | tf_op jit(solution)/shard_map/ppermute | solution.py:20
  160.7 55.2 %copy-start.1 = (s32[32,8]{0,1:T(8,128)S(1)}, s32[32,8]{0,1:T(8,128)}, u32[]{:S(2)}) copy-start(s32[32,8]{0,1:T(8,128)} %param.7) | copy-start | bytes 3076
  211.1 94.4 %collective-permute-start.5 = (bf16[2048,1024]{1,0:T(8,128)(2,1)}, bf16[2048,1024]{1,0:T(8,128)(2,1)}, u32[]{:S(2)}, u32[]{:S(2)}) collective-permute-start(bf16[2048,1024]{1,0:T(8,128)(2,1)} %maximum_select_fusion.6), channel_id=1, source_target_pairs={{0,256},{8,264},{16,272},{24,280},{32,288},{40,296},{48,304},{56,3... | collective-permute-start | bytes 12582920 | tf_op jit(solution)/shard_map/ppermute | solution.py:20
  312.6 7.2 %collective-permute-start.6 = (bf16[16,256]{1,0:T(8,128)(2,1)S(1)}, bf16[16,256]{1,0:T(8,128)(2,1)S(1)}, u32[]{:S(2)}, u32[]{:S(2)}) collective-permute-start(bf16[16,256]{1,0:T(8,128)(2,1)S(1)} %get-tuple-element.11), channel_id=1, source_target_pairs={{0,1},{1,2},{2,3},{3,4},{4,5},{5,6},{6,7},{8,9},{9,10},{10,11},{11... | collective-permute-start | bytes 24584 | tf_op jit(solution)/shard_map/ppermute | solution.py:36
  317.9 5.0 %collective-permute-start.7 = (bf16[16,256]{1,0:T(8,128)(2,1)S(1)}, bf16[16,256]{1,0:T(8,128)(2,1)S(1)}, u32[]{:S(2)}, u32[]{:S(2)}) collective-permute-start(bf16[16,256]{1,0:T(8,128)(2,1)S(1)} %get-tuple-element.12), channel_id=1, source_target_pairs={{1,0},{2,1},{3,2},{4,3},{5,4},{6,5},{7,6},{9,8},{10,9},{11,10},{12... | collective-permute-start | bytes 24584 | tf_op jit(solution)/shard_map/ppermute | solution.py:39
  329.5 4.3 %collective-permute-start.8 = (bf16[16,256]{1,0:T(8,128)(2,1)S(1)}, bf16[16,256]{1,0:T(8,128)(2,1)S(1)}, u32[]{:S(2)}, u32[]{:S(2)}) collective-permute-start(bf16[16,256]{1,0:T(8,128)(2,1)S(1)} %get-tuple-element.9), channel_id=1, source_target_pairs={{0,1},{1,2},{2,3},{3,4},{4,5},{5,6},{6,7},{8,9},{9,10},{10,11},{11... | collective-permute-start | bytes 24584 | tf_op jit(solution)/shard_map/ppermute | solution.py:36
  331.4 5.0 %collective-permute-start.9 = (bf16[16,256]{1,0:T(8,128)(2,1)S(1)}, bf16[16,256]{1,0:T(8,128)(2,1)S(1)}, u32[]{:S(2)}, u32[]{:S(2)}) collective-permute-start(bf16[16,256]{1,0:T(8,128)(2,1)S(1)} %get-tuple-element.10), channel_id=1, source_target_pairs={{1,0},{2,1},{3,2},{4,3},{5,4},{6,5},{7,6},{9,8},{10,9},{11,10},{12... | collective-permute-start | bytes 24584 | tf_op jit(solution)/shard_map/ppermute | solution.py:39
  343.0 4.3 %collective-permute-start.10 = (bf16[16,256]{1,0:T(8,128)(2,1)S(1)}, bf16[16,256]{1,0:T(8,128)(2,1)S(1)}, u32[]{:S(2)}, u32[]{:S(2)}) collective-permute-start(bf16[16,256]{1,0:T(8,128)(2,1)S(1)} %get-tuple-element.7), channel_id=1, source_target_pairs={{0,1},{1,2},{2,3},{3,4},{4,5},{5,6},{6,7},{8,9},{9,10},{10,11},{11... | collective-permute-start | bytes 24584 | tf_op jit(solution)/shard_map/ppermute | solution.py:36
  345.0 5.0 %collective-permute-start.11 = (bf16[16,256]{1,0:T(8,128)(2,1)S(1)}, bf16[16,256]{1,0:T(8,128)(2,1)S(1)}, u32[]{:S(2)}, u32[]{:S(2)}) collective-permute-start(bf16[16,256]{1,0:T(8,128)(2,1)S(1)} %get-tuple-element.8), channel_id=1, source_target_pairs={{1,0},{2,1},{3,2},{4,3},{5,4},{6,5},{7,6},{9,8},{10,9},{11,10},{12... | collective-permute-start | bytes 24584 | tf_op jit(solution)/shard_map/ppermute | solution.py:39
  356.6 4.3 %collective-permute-start.12 = (bf16[16,256]{1,0:T(8,128)(2,1)S(1)}, bf16[16,256]{1,0:T(8,128)(2,1)S(1)}, u32[]{:S(2)}, u32[]{:S(2)}) collective-permute-start(bf16[16,256]{1,0:T(8,128)(2,1)S(1)} %get-tuple-element.5), channel_id=1, source_target_pairs={{0,1},{1,2},{2,3},{3,4},{4,5},{5,6},{6,7},{8,9},{9,10},{10,11},{11... | collective-permute-start | bytes 24584 | tf_op jit(solution)/shard_map/ppermute | solution.py:36
  358.6 5.0 %collective-permute-start.13 = (bf16[16,256]{1,0:T(8,128)(2,1)S(1)}, bf16[16,256]{1,0:T(8,128)(2,1)S(1)}, u32[]{:S(2)}, u32[]{:S(2)}) collective-permute-start(bf16[16,256]{1,0:T(8,128)(2,1)S(1)} %get-tuple-element.6), channel_id=1, source_target_pairs={{1,0},{2,1},{3,2},{4,3},{5,4},{6,5},{7,6},{9,8},{10,9},{11,10},{12... | collective-permute-start | bytes 24584 | tf_op jit(solution)/shard_map/ppermute | solution.py:39
